TPU v7x, 32 devices: a whole 2x2x4 slice. The times are simulated.
32 devices in a mesh: mem: 8 (over z, core), slab: 4 (over y, x).
Axes of the slice: x: 2, y: 2, z: 4, core: 2. Of those that a mesh axis runs over, the one named last changes fastest.
Arguments:
- thickness: float32 [64, 256, 384], P('mem', 'slab'), may hold values from 0.5 to 2.5
- face_u: float32 [256, 384], P('slab'), may hold values from -0.4 to 0.4
- face_v: float32 [256, 384], P('slab'), may hold values from -0.4 to 0.4
- obs_cells: int32 [512, 4], P('slab'), may hold values from 0 to 98303, as said below
- obs_weights: int32 [512, 4], P('slab'), may hold values from 1 to 4
- obs_values: float32 [512], P('slab'), may hold values from -6 to 6
- obs_noise: float32 [64, 512], P('mem', 'slab'), may hold values from -3 to 3
- cov_inverse: float32 [512, 512], P('slab'), may hold values from -0.375 to 0.375
- taper_mask: int32 [4, 4], replicated, may hold values from 0 to 1, as said below
Outputs:
- analysis: float32 [64, 256, 384], P('mem', 'slab')
Inputs may be any that keep to these rules, and one draw needn't show every extreme that they name: `obs_cells`: observation o covers a 2 x 2 square of cells, all within the rows of slab o // 128. `taper_mask`: entries are 0 or 1 and the diagonal is 1.
All inputs are finite; a program needn't handle non-finite values.
Results may differ from a plain program's by a relative error of at most 0.0003.
Values sent between devices are 32-bit elements; how exact they have to be, the bound alone decides.
A program may use at most 64 MiB of HBM per device.

v0:
```python
import jax
import jax.numpy as jnp
from jax import lax
from jax.sharding import PartitionSpec as P


def padded_2(block, sides, width):
    for axis, dim in sides:
        count = lax.axis_size(axis)
        forward = [(i, i + 1) for i in range(count - 1)]
        backward = [(target, source) for source, target in forward]
        low = lax.ppermute(
            lax.slice_in_dim(block, block.shape[dim] - width, None, axis=dim), axis, forward
        )
        high = lax.ppermute(lax.slice_in_dim(block, 0, width, axis=dim), axis, backward)
        block = jnp.concatenate([low, block, high], axis=dim)
    return block


def minmod(first_diff, second_diff):
    return (
        0.5
        * (jnp.sign(first_diff) + jnp.sign(second_diff))
        * jnp.minimum(jnp.abs(first_diff), jnp.abs(second_diff))
    )


def face_flux(padded, velocity, axis_dim):
    counted = padded.shape[axis_dim] - 3
    far_low = lax.slice_in_dim(padded, 0, counted, axis=axis_dim)
    near_low = lax.slice_in_dim(padded, 1, 1 + counted, axis=axis_dim)
    near_high = lax.slice_in_dim(padded, 2, 2 + counted, axis=axis_dim)
    far_high = lax.slice_in_dim(padded, 3, 3 + counted, axis=axis_dim)
    left_state = near_low + 0.5 * minmod(near_low - far_low, near_high - near_low)
    right_state = near_high - 0.5 * minmod(near_high - near_low, far_high - near_high)
    return jnp.maximum(velocity, 0.0) * left_state + jnp.minimum(velocity, 0.0) * right_state


def local(
    thickness,
    face_u,
    face_v,
    obs_cells,
    obs_weights,
    obs_values,
    obs_noise,
    cov_inverse,
    taper_mask,
):
    member_subset = thickness.shape[0]
    band_rows = thickness.shape[1]
    column_list = thickness.shape[2]
    slab_index = lax.axis_index("slab")
    stacked = jnp.concatenate([thickness, face_v[None]], 0)
    padded = padded_2(stacked, (("slab", 1),), 2)
    row_pad = padded[:member_subset]
    row_speed = padded[member_subset, 2 : band_rows + 3]
    row_fluxes = face_flux(row_pad, row_speed, 1)
    col_pad = jnp.pad(thickness, ((0, 0), (0, 0), (2, 2)))
    col_speed = jnp.pad(face_u, ((0, 0), (0, 1)))
    column_fluxes = face_flux(col_pad, col_speed, 2)
    prior_state = (
        thickness
        - (column_fluxes[:, :, 1:] - column_fluxes[:, :, :-1])
        - (row_fluxes[:, 1:, :] - row_fluxes[:, :-1, :])
    )
    state_vector = prior_state.reshape(member_subset, band_rows * column_list)
    local_cells = obs_cells - slab_index * (band_rows * column_list)
    weights = obs_weights.astype(jnp.float32)
    picked = state_vector[:, local_cells]
    obs_model = jnp.sum(picked * weights[None], -1) / jnp.sum(weights, -1)[None]
    innovation = obs_values[None, :] + obs_noise - obs_model
    white_terms = jnp.dot(innovation, cov_inverse, precision=lax.Precision.HIGHEST)
    whitened = lax.psum_scatter(white_terms, "slab", scatter_dimension=1, tiled=True)
    model_all, white_all = (
        lax.all_gather(obs_model, "mem", axis=0, tiled=True),
        lax.all_gather(whitened, "mem", axis=0, tiled=True),
    )
    obs_mean = jnp.mean(model_all, 0, keepdims=True)
    cell_state = lax.all_to_all(state_vector, "mem", split_axis=1, concat_axis=0, tiled=True)
    members = cell_state.shape[0]
    anomaly = cell_state - jnp.mean(cell_state, 0, keepdims=True)
    obs_anomaly = model_all - obs_mean
    anom_full, white_full = (
        lax.all_gather(obs_anomaly, "slab", axis=1, tiled=True),
        lax.all_gather(white_all, "slab", axis=1, tiled=True),
    )
    block_size = obs_anomaly.shape[1]
    mask_row = lax.dynamic_slice_in_dim(taper_mask, slab_index, 1, 0)[0].astype(jnp.float32)
    taper_row = jnp.repeat(mask_row, block_size)
    cross = lax.dot_general(
        anomaly, anom_full, (((0,), (0,)), ((), ())), precision=lax.Precision.HIGHEST
    ) / (members - 1)
    tapered = cross * taper_row[None, :]
    update = lax.dot_general(
        white_full, tapered, (((1,), (1,)), ((), ())), precision=lax.Precision.HIGHEST
    )
    analysis_cells = cell_state + update
    returned = lax.all_to_all(analysis_cells, "mem", split_axis=0, concat_axis=1, tiled=True)
    return returned.reshape(member_subset, band_rows, column_list)


def solution(mesh):
    return jax.shard_map(
        local,
        mesh=mesh,
        in_specs=(
            P("mem", "slab", None),
            P("slab", None),
            P("slab", None),
            P("slab", None),
            P("slab", None),
            P("slab"),
            P("mem", "slab"),
            P("slab", None),
            P(),
        ),
        out_specs=P("mem", "slab", None),
        check_vma=False,
    )
```

profile of v0, /device:TPU:0, one launch (start us, length us, event | category | flops | bytes accessed | tf_op | source)
XLA Modules:
  0.0 138.8 jit_solution(13175700690734752969)
XLA Ops:
  6.5 0.0 copy-start
  6.5 0.0 copy-start.1
  6.5 1.1 pad_maximum_fusion.3
  7.6 1.3 collective-permute-start
  8.9 5.5 %collective-permute-start.1 = (f32[9,2,384]{2,1,0:T(2,128)S(1)}, f32[9,2,384]{2,1,0:T(2,128)S(1)}, u32[]{:S(2)}, u32[]{:S(2)}) collective-permute-start(f32[9,2,384]{2,1,0:T(2,128)S(1)} %get-tuple-element.9), channel_id=1, source_target_pairs={{0,1},{1,2},{2,3},{4,5},{5,6},{6,7},{8,9},{9,10},{10,11},{12,13},{... | collective-permute-start | bytes 82952 | tf_op jit(solution)/shard_map/ppermute | solution.py:12
  14.4 0.9 pad_maximum_fusion.1
  15.4 0.7 compare_select_fusion
  16.1 0.1 copy.36
  16.2 0.1 reshape.37
  16.3 3.6 %multiply_add_fusion = f32[8,64,385]{2,1,0:T(8,128)S(1)} fusion(f32[8,64,384]{2,1,0:T(8,128)} %param.9, f32[64,385]{1,0:T(8,128)S(1)} %get-tuple-element.12, f32[64,385]{1,0:T(8,128)S(1)} %get-tuple-element.11), kind=kLoop, calls=%fused_computation.12 | loop fusion | flops 4730880 | bytes 1772032 | tf_op jit(solution)/shard_map/add | solution.py:36
  19.9 0.7 convert_reduce_fusion
  20.6 0.0 collective-permute-done
  20.6 0.9 maximum_bitcast_fusion
  21.6 0.0 collective-permute-done.1
  21.6 1.6 %maximum_maximum_fusion = (f32[9,66,384]{2,1,0:T(8,128)S(1)}, f32[9,66,384]{2,1,0:T(8,128)S(1)}) fusion(f32[1,64,384]{2,1,0:T(8,128)} %bitcast.30, f32[8,64,384]{2,1,0:T(8,128)} %param.9, f32[9,2,384]{2,1,0:T(2,128)S(1)} %collective-permute-done.1, f32[9,2,384]{2,1,0:T(2,128)S(1)} %collective-permute-done), kind=kLoop, calls=%fused_computation.14 | loop fusion | flops 912384 | bytes 2764800 | tf_op jit(solution)/shard_map/concatenate | solution.py:16
  23.2 0.0 copy-start.2
  23.2 1.3 multiply_add_fusion.1
  24.5 0.0 copy-done.1
  24.5 0.3 fusion.11
  24.9 0.1 all_to_all.26
  25.0 1.3 copy.34
  26.4 5.4 %all-to-all-start = ((f32[8,8,3072]{2,0,1:T(8,128)}), f32[8,8,3072]{2,0,1:T(8,128)S(1)}, u32[]{:S(2)}, u32[]{:S(2)}) async-start(f32[8,8,3072]{2,0,1:T(8,128)} %copy.34), calls=%async_computation | async-start | bytes 1572864 | tf_op jit(solution)/shard_map/all_to_all | solution.py:80
  31.8 0.0 reduce-scatter.2.cloned.1.call-start
  31.8 0.7 multiply_bitcast_fusion
  32.5 0.0 copy-done.2
  32.5 0.1 copy.37
  32.6 0.1 broadcast_bitcast_fusion
  32.7 0.0 copy-start.3
  32.7 0.0 copy-start.4
  32.7 6.6 %copy.35 = f32[8,64,384]{0,2,1:T(8,128)} copy(f32[8,64,384]{2,1,0:T(8,128)S(1)} %fusion.11) | data formatting | bytes 1572864 | tf_op jit(solution)/shard_map/sub | solution.py:63
  39.2 5.6 %gather_fusion = f32[512,8]{1,0:T(8,128)S(1)} fusion(f32[8,24576]{0,1:T(8,128)} %bitcast.25, s32[1024]{0:T(1024)S(1)} %pad_clamp_fusion), kind=kCustom, calls=%fused_computation | custom fusion | bytes 34816 | tf_op jit(solution)/shard_map/gather | solution.py:70
  44.9 0.2 multiply_reduce_fusion
  45.2 0.0 copy-done
  45.2 0.0 copy-done.3
  45.2 0.0 copy-done.4
  45.2 0.8 fusion.15
  46.0 0.0 reduce-scatter.2.cloned.1.call-update
  46.1 14.6 %all_gather.14 = f32[64,128]{1,0:T(8,128)S(1)} all-gather(f32[8,128]{1,0:T(8,128)S(1)} %divide_bitcast_fusion), channel_id=1, replica_groups=mesh['mem'=8,'slab'=4] {'mem'}, dimensions={0}, use_global_device_ids=true | all-gather | bytes 36864 | tf_op jit(solution)/shard_map/all_gather | solution.py:76
  60.7 9.9 %all_gather.15 = f32[64,512]{1,0:T(8,128)S(1)} all-gather(f32[64,128]{1,0:T(8,128)S(1)} %broadcast_subtract_fusion), channel_id=1, replica_groups=mesh['mem'=8,'slab'=4] {'slab'}, dimensions={1}, use_global_device_ids=true | all-gather | bytes 163840 | tf_op jit(solution)/shard_map/all_gather | solution.py:85
  70.6 0.0 reduce-scatter.2.cloned.1.call-done
  70.6 14.2 %all_gather.12 = f32[64,128]{1,0:T(8,128)S(1)} all-gather(f32[8,128]{1,0:T(8,128)} %reduce-scatter.2.cloned.1.call-done), channel_id=1, replica_groups=mesh['mem'=8,'slab'=4] {'mem'}, dimensions={0}, use_global_device_ids=true | all-gather | bytes 36864 | tf_op jit(solution)/shard_map/all_gather | solution.py:77
  84.7 9.0 %all_gather.13 = f32[64,512]{1,0:T(8,128)S(1)} all-gather(f32[64,128]{1,0:T(8,128)S(1)} %all_gather.12), channel_id=1, replica_groups=mesh['mem'=8,'slab'=4] {'slab'}, dimensions={1}, use_global_device_ids=true | all-gather | bytes 163840 | tf_op jit(solution)/shard_map/all_gather | solution.py:86
  93.8 0.0 all-to-all-done
  93.8 0.1 reduce_sum.38
  93.8 5.2 %fusion.13 = f32[3072,512]{1,0:T(8,128)S(1)} fusion(f32[64,512]{1,0:T(8,128)S(1)} %all_gather.15, f32[8,8,3072]{2,0,1:T(8,128)S(1)} %all-to-all-done, f32[3072]{0:T(1024)S(1)} %broadcast_multiply_fusion), kind=kOutput, calls=%fused_computation.23 | convolution fusion | flops 1208156160 | bytes 7221248 | tf_op jit(solution)/shard_map/dot_general | solution.py:91
  99.0 6.0 %fusion.5 = f32[8,8,3072]{2,1,0:T(8,128)S(1)} fusion(f32[64,512]{1,0:T(8,128)S(1)} %all_gather.13, f32[3072,512]{1,0:T(8,128)S(1)} %fusion.13, f32[512]{0:T(512)S(1)} %broadcast_bitcast_fusion, f32[8,8,3072]{2,0,1:T(8,128)S(1)} %all-to-all-done), kind=kOutput, calls=%fused_computation.4 | convolution fusion | flops 1209729024 | bytes 7997440 | tf_op jit(solution)/shard_map/dot_general | solution.py:95
  105.1 25.4 %all_to_all.35 = f32[8,8,3072]{2,1,0:T(8,128)S(1)} all-to-all(f32[8,8,3072]{2,1,0:T(8,128)S(1)} %fusion.5), channel_id=1, replica_groups=mesh['mem'=8,'slab'=4] {'mem'}, dimensions={0} | all-to-all | bytes 1572864 | tf_op jit(solution)/shard_map/all_to_all | solution.py:99
  130.5 0.5 copy.39
  130.9 1.0 reshape.34
  (9 shorter events, 0.1 us)
Async XLA Ops:
  6.5 38.6 %copy-start = (f32[128,512]{1,0:T(8,128)S(1)}, f32[128,512]{1,0:T(8,128)}, u32[]{:S(2)}) copy-start(f32[128,512]{1,0:T(8,128)} %param.16) | copy-start | bytes 786436
  6.5 18.0 %copy-start.1 = (f32[8,64,384]{2,1,0:T(8,128)S(1)}, f32[8,64,384]{2,1,0:T(8,128)}, u32[]{:S(2)}) copy-start(f32[8,64,384]{2,1,0:T(8,128)} %param.9) | copy-start | bytes 2359300
  7.6 13.0 %collective-permute-start = (f32[9,2,384]{2,1,0:T(2,128)S(1)}, f32[9,2,384]{2,1,0:T(2,128)S(1)}, u32[]{:S(2)}, u32[]{:S(2)}) collective-permute-start(f32[9,2,384]{2,1,0:T(2,128)S(1)} %get-tuple-element.10), channel_id=1, source_target_pairs={{1,0},{2,1},{3,2},{5,4},{6,5},{7,6},{9,8},{10,9},{11,10},{13,12},{... | collective-permute-start | bytes 82952 | tf_op jit(solution)/shard_map/ppermute | solution.py:15
  8.9 12.6 %collective-permute-start.1 = (f32[9,2,384]{2,1,0:T(2,128)S(1)}, f32[9,2,384]{2,1,0:T(2,128)S(1)}, u32[]{:S(2)}, u32[]{:S(2)}) collective-permute-start(f32[9,2,384]{2,1,0:T(2,128)S(1)} %get-tuple-element.9), channel_id=1, source_target_pairs={{0,1},{1,2},{2,3},{4,5},{5,6},{6,7},{8,9},{9,10},{10,11},{12,13},{... | collective-permute-start | bytes 82952 | tf_op jit(solution)/shard_map/ppermute | solution.py:12
  23.2 9.3 %copy-start.2 = (s32[128,4]{0,1:T(4,128)S(1)}, s32[128,4]{0,1:T(4,128)}, u32[]{:S(2)}) copy-start(s32[128,4]{0,1:T(4,128)} %param.13) | copy-start | bytes 6148
  26.4 67.4 %all-to-all-start = ((f32[8,8,3072]{2,0,1:T(8,128)}), f32[8,8,3072]{2,0,1:T(8,128)S(1)}, u32[]{:S(2)}, u32[]{:S(2)}) async-start(f32[8,8,3072]{2,0,1:T(8,128)} %copy.34), calls=%async_computation | async-start | bytes 1572864 | tf_op jit(solution)/shard_map/all_to_all | solution.py:80
  31.8 38.8 %reduce-scatter.2.cloned.1.call-start = ((), (), s32[]{:S(2)}) async-start(), calls=%async_computation.3 | async-start | bytes 20480 | tf_op jit(solution)/shard_map/reduce_scatter | solution.py:74
  32.7 12.5 %copy-start.3 = (f32[8,128]{1,0:T(8,128)S(1)}, f32[8,128]{1,0:T(8,128)}, u32[]{:S(2)}) copy-start(f32[8,128]{1,0:T(8,128)} %param.15) | copy-start | bytes 12292
  32.7 12.5 %copy-start.4 = (f32[128]{0:T(128)S(1)}, f32[128]{0:T(128)}, u32[]{:S(2)}) copy-start(f32[128]{0:T(128)} %param.14) | copy-start | bytes 1540
Sparse Core Ops, SparseCore 0:
  46.2 24.1 reduce-scatter.1
where the time goes:
time: 139 us
  blocking collectives  73.1 us (53%)
  local copies, waits for them, and re-layouts  15.6 us (11%)
  between operations  13.6 us (10%)
  other arithmetic  12.3 us (9%)
  starting transfers between devices  12.2 us (9%)
  matrix products  12.1 us (9%)
    all_to_all x1, blocking collectives, local(): lax.all_to_all(analysis_cells, 'mem', split_axis=0, concat_axis=1, tiled=...  25.4 us
    all_gather x1, blocking collectives, local(): lax.all_gather(obs_model, 'mem', axis=0, tiled=True)  14.6 us
    all_gather x1, blocking collectives, local(): lax.all_gather(whitened, 'mem', axis=0, tiled=True)  14.2 us
    all_gather x1, blocking collectives, local(): lax.all_gather(obs_anomaly, 'slab', axis=1, tiled=True)  9.86 us
    all_gather x1, blocking collectives, local(): lax.all_gather(white_all, 'slab', axis=1, tiled=True)  9 us
    sub x1, local copies, waits for them, and re-layouts, local(): thickness - (column_fluxes[:, :, 1:] - column_fluxes[:, :, :-1])  6.56 us
    dot_general x1, matrix products, local(): lax.dot_general(white_full, tapered, (((1,), (1,)), ((), ())), precision=...  6.04 us
    gather x1, local copies, waits for them, and re-layouts, local(): picked = state_vector[:, local_cells]  5.6 us
  transfers between devices with their start and end apart: 4, of which 0 were waited for; matrix products, arithmetic and copies ran while one was open for 15% of the time, Pallas kernels for 0%

commit v1 on v0

v1 whole, which is shorter than its diff:
```python
import functools

import jax
import jax.numpy as jnp
from jax import lax
from jax.experimental import pallas as pl
from jax.experimental.pallas import tpu as pltpu
from jax.sharding import PartitionSpec as P

MESH = pl.DeviceIdType.MESH
F32 = jnp.float32
BF16 = jnp.bfloat16


def minmod(a, b):
    return jnp.maximum(jnp.minimum(a, b), 0.0) + jnp.minimum(jnp.maximum(a, b), 0.0)


def split_blocks(rows, cols, n_mem):
    for nc in range(1, n_mem + 1):
        if n_mem % nc == 0 and cols % (128 * nc) == 0 and rows % (n_mem // nc) == 0:
            return nc, rows // (n_mem // nc)
    raise ValueError("no split")


def kernel(
    n_mem, n_slab, nc, rc,
    x_ref, u_ref, v_ref, cells_ref, wts_ref, vals_ref, noise_ref, cinv_ref, taper_ref,
    res_ref,
    t_buf, v_buf, up_buf, dn_buf, hi_rx, lo_rx, fblk, gath, outb, s_buf, rw_buf,
    om_all, p_buf, p_rx, b_buf, x_all,
    halo_s, halo_r, f_s, f_r, o_s, o_r, p_s, p_r, b_s, b_r, x_s, x_r, r_s, r_r,
):
    ng = n_mem // nc
    rows, cols = u_ref.shape
    ml = noise_ref.shape[0]
    cc = cols // nc
    ob = noise_ref.shape[1]
    members = n_mem * ml
    me = lax.axis_index("mem")
    sl = lax.axis_index("slab")
    my_g = me // nc
    my_c = me % nc
    up = lax.rem(sl + 1, n_slab)
    down = lax.rem(sl + n_slab - 1, n_slab)

    barrier = pltpu.get_barrier_semaphore()
    for k in range(1, n_mem):
        pl.semaphore_signal(barrier, inc=1, device_id=(lax.rem(me + k, n_mem), sl), device_id_type=MESH)
    for k in range(1, n_slab):
        pl.semaphore_signal(barrier, inc=1, device_id=(me, lax.rem(sl + k, n_slab)), device_id_type=MESH)

    tr = 8

    def load_rows(i, carry):
        r = pl.multiple_of(i * tr, tr)
        t_buf[pl.ds(r + 2, tr)] = jnp.swapaxes(x_ref[:, pl.ds(r, tr), :], 0, 1)
        return carry

    lax.fori_loop(0, rows // tr, load_rows, 0)
    for r in range(2):
        up_buf[r] = t_buf[2 + r]
        dn_buf[r] = t_buf[rows + r]
    up_buf[2] = jnp.broadcast_to(v_ref[pl.ds(0, 1), :], (ml, cols))
    v_buf[0:rows, :] = v_ref[...]

    pl.semaphore_wait(barrier, n_mem - 1 + n_slab - 1)

    def halo_copy(i, src, dst, target):
        return pltpu.make_async_remote_copy(
            src_ref=src, dst_ref=dst, send_sem=halo_s.at[i], recv_sem=halo_r.at[i],
            device_id=(me, target), device_id_type=MESH)

    to_down = halo_copy(0, up_buf, hi_rx, down)
    to_up = halo_copy(1, dn_buf, lo_rx, up)
    to_down.start()
    to_up.start()

    lane = lax.broadcasted_iota(jnp.int32, (ml, cols), 1)
    first_lane = lane == 0
    last_lane = lane == cols - 1

    def from_left(a):
        return jnp.where(first_lane, 0.0, pltpu.roll(a, 1, 1))

    def from_right(a):
        return jnp.where(last_lane, 0.0, pltpu.roll(a, cols - 1, 1))

    def compute(g):
        r0 = g * rc
        hm2, hm1, h0, h1 = (t_buf[r0 + i] for i in range(4))
        s_low = minmod(hm1 - hm2, h0 - hm1)
        s = minmod(h0 - hm1, h1 - h0)
        w = v_buf[pl.ds(r0, 1), :]
        flux = jnp.maximum(w, 0.0) * (hm1 + 0.5 * s_low) + jnp.minimum(w, 0.0) * (h0 - 0.5 * s)
        for r in range(rc):
            h2 = t_buf[r0 + r + 4]
            s1 = minmod(h1 - h0, h2 - h1)
            w = v_buf[pl.ds(r0 + r + 1, 1), :]
            flux1 = jnp.maximum(w, 0.0) * (h0 + 0.5 * s) + jnp.minimum(w, 0.0) * (h1 - 0.5 * s1)
            u = u_ref[pl.ds(r0 + r, 1), :]
            d = h0 - from_left(h0)
            d1 = from_right(h0) - h0
            sc = 0.5 * minmod(d, d1)
            fc = jnp.maximum(u, 0.0) * from_left(h0 + sc) + jnp.minimum(u, 0.0) * (h0 - sc)
            f = h0 - (from_right(fc) - fc) - (flux1 - flux)
            for ci in range(nc):
                fblk[g, ci, r] = f[:, ci * cc:(ci + 1) * cc]
            h0, h1, s, flux = h1, h2, s1, flux1

    def fwd_copy(g, ci, t, slot):
        return pltpu.make_async_remote_copy(
            src_ref=fblk.at[g, ci], dst_ref=gath.at[slot], send_sem=f_s.at[t], recv_sem=f_r.at[slot],
            device_id=(t, sl), device_id_type=MESH)

    def send_group(g):
        for ci in range(nc):
            t = g * nc + ci

            @pl.when(t != me)
            def _():
                fwd_copy(g, ci, t, me).start()

    def inner(k, carry):
        g = lax.rem(my_g + k, ng)

        @pl.when(jnp.logical_and(g >= 1, g <= ng - 2))
        def _():
            compute(g)
            send_group(g)

        return carry

    lax.fori_loop(1, ng + 1, inner, 0)

    base = (sl * (rows * cols)).astype(F32)
    local_cells = cells_ref[...].astype(F32) - base
    cell_row = jnp.floor((local_cells + 0.5) * (1.0 / cols))
    cell_col = local_cells - cell_row * cols
    weights = wts_ref[...].astype(F32)
    w_sum = jnp.sum(weights, axis=0, keepdims=True)
    col_min = jnp.min(cell_col, axis=0, keepdims=True)
    col_iota = lax.broadcasted_iota(jnp.int32, (cols, ob), 0).astype(F32)
    row_iota = lax.broadcasted_iota(jnp.int32, (rows, ob), 0).astype(F32)
    onehot = []
    for b in range(2):
        onehot.append((col_iota == col_min + float(b)).astype(F32))
        total = jnp.zeros((rows, ob), F32)
        for k in range(cells_ref.shape[0]):
            wk = jnp.where(cell_col[k:k + 1] == col_min + float(b), weights[k:k + 1], 0.0)
            total += jnp.where(row_iota == cell_row[k:k + 1], wk, 0.0)
        rw_buf[:, b * ob:(b + 1) * ob] = total
    onehot = jnp.concatenate(onehot, axis=1).astype(BF16)

    to_down.wait_recv()
    to_up.wait_recv()
    low_edge = sl == 0
    high_edge = sl == n_slab - 1
    for r in range(2):
        t_buf[r] = jnp.where(low_edge, 0.0, lo_rx[r])
        t_buf[rows + 2 + r] = jnp.where(high_edge, 0.0, hi_rx[r])
    v_buf[rows:rows + 8, :] = jnp.broadcast_to(jnp.where(high_edge, 0.0, hi_rx[2])[0:1], (8, cols))
    compute(0)
    compute(ng - 1)

    s_total = None
    for ci in range(nc):
        f = fblk[:, ci].reshape(rows * ml, cc)
        f_hi = f.astype(BF16)
        f_lo = (f - f_hi.astype(F32)).astype(BF16)
        q = onehot[ci * cc:(ci + 1) * cc]
        part = jnp.dot(f_hi, q, preferred_element_type=F32) + jnp.dot(f_lo, q, preferred_element_type=F32)
        s_total = part if s_total is None else s_total + part
    s_buf[...] = s_total

    acc = jnp.zeros((ml, 2 * ob), F32)
    for r in range(rows):
        acc += s_buf[r * ml:(r + 1) * ml, :] * rw_buf[r:r + 1, :]
    obs_model = (acc[:, :ob] + acc[:, ob:]) / w_sum
    om_all[me] = obs_model

    def bcast(buf, slot, i, t_mem, t_slab, ss, rs):
        return pltpu.make_async_remote_copy(
            src_ref=buf.at[slot], dst_ref=buf.at[slot], send_sem=ss.at[i], recv_sem=rs.at[slot],
            device_id=(t_mem, t_slab), device_id_type=MESH)

    mem_mates = [lax.rem(me + k, n_mem) for k in range(1, n_mem)]
    slab_mates = [lax.rem(sl + k, n_slab) for k in range(1, n_slab)]

    for t in mem_mates:
        bcast(om_all, me, t, t, sl, o_s, o_r).start()

    innovation = vals_ref[...] + noise_ref[...] - obs_model
    white_terms = jnp.dot(innovation, cinv_ref[...], preferred_element_type=F32, precision=lax.Precision.HIGHEST)
    for b in range(n_slab):
        p_buf[b] = white_terms[:, b * ob:(b + 1) * ob]
    p_rx[sl] = p_buf[sl]

    def p_copy(b, slot):
        return pltpu.make_async_remote_copy(
            src_ref=p_buf.at[b], dst_ref=p_rx.at[slot], send_sem=p_s.at[b], recv_sem=p_r.at[slot],
            device_id=(me, b), device_id_type=MESH)

    for b in slab_mates:
        p_copy(b, sl).start()

    send_group(0)
    send_group(ng - 1)
    gath[me] = fblk[my_g, my_c]

    for b in slab_mates:
        p_copy(b, b).wait_recv()
    whitened = p_rx[0]
    for b in range(1, n_slab):
        whitened += p_rx[b]
    for t in mem_mates:
        bcast(om_all, t, t, t, sl, o_s, o_r).wait_recv()
    om = om_all[...].reshape(members, ob)
    obs_anomaly = om - jnp.sum(om, axis=0, keepdims=True) * (1.0 / members)
    b_buf[sl] = lax.dot_general(
        whitened, obs_anomaly, (((1,), (1,)), ((), ())),
        preferred_element_type=F32, precision=lax.Precision.HIGHEST)
    for b in slab_mates:
        bcast(b_buf, sl, b, me, b, b_s, b_r).start()
    for b in slab_mates:
        bcast(b_buf, b, b, me, b, b_s, b_r).wait_recv()
    ens = jnp.zeros((ml, members), F32)
    for b in range(n_slab):
        ens += taper_ref[sl, b].astype(F32) * b_buf[b]
    ens = ens - jnp.sum(ens, axis=1, keepdims=True) * (1.0 / members)
    x_all[me] = ens * (1.0 / (members - 1))
    for t in mem_mates:
        bcast(x_all, me, t, t, sl, x_s, x_r).start()

    for t in mem_mates:
        fwd_copy(my_g, my_c, t, t).wait_recv()
    for t in mem_mates:
        bcast(x_all, t, t, t, sl, x_s, x_r).wait_recv()

    xm = x_all[...].reshape(members, members)
    x_hi = xm.astype(BF16).astype(F32)
    lhs = jnp.concatenate([x_hi, x_hi, xm - x_hi], axis=1).astype(BF16)
    for r in range(rc):
        g = gath[:, r].reshape(members, cc)
        g_hi = g.astype(BF16)
        g_lo = (g - g_hi.astype(F32)).astype(BF16)
        rhs = jnp.concatenate([g_hi, g_lo, g_hi], axis=0)
        out = g + jnp.dot(lhs, rhs, preferred_element_type=F32)
        outb[:, r] = out.reshape(n_mem, ml, cc)

    def rev_copy(t, g, ci, slot):
        return pltpu.make_async_remote_copy(
            src_ref=outb.at[t], dst_ref=res_ref.at[g, ci], send_sem=r_s.at[t], recv_sem=r_r.at[slot],
            device_id=(t, sl), device_id_type=MESH)

    for t in mem_mates:
        rev_copy(t, my_g, my_c, me).start()
    res_ref[my_g, my_c] = outb[me]

    to_down.wait_send()
    to_up.wait_send()
    for b in slab_mates:
        p_copy(b, sl).wait_send()
        bcast(b_buf, sl, b, me, b, b_s, b_r).wait_send()
    for t in mem_mates:
        bcast(om_all, me, t, t, sl, o_s, o_r).wait_send()
        bcast(x_all, me, t, t, sl, x_s, x_r).wait_send()
        fwd_copy(t // nc, t % nc, t, me).wait_send()
    for t in mem_mates:
        rev_copy(t, my_g, my_c, me).wait_send()
    for t in mem_mates:
        rev_copy(t, t // nc, t % nc, t).wait_recv()


def local(n_mem, n_slab, thickness, face_u, face_v, obs_cells, obs_weights, obs_values, obs_noise, cov_inverse,
          taper_mask):
    ml, rows, cols = thickness.shape
    ob = obs_values.shape[0]
    members = ml * n_mem
    nc, rc = split_blocks(rows, cols, n_mem)
    ng, cc = n_mem // nc, cols // nc
    vmem = pl.BlockSpec(memory_space=pltpu.VMEM)
    dma = pltpu.SemaphoreType.DMA
    out = pl.pallas_call(
        functools.partial(kernel, n_mem, n_slab, nc, rc),
        out_shape=jax.ShapeDtypeStruct((ng, nc, rc, ml, cc), F32),
        in_specs=[vmem] * 8 + [pl.BlockSpec(memory_space=pltpu.SMEM)],
        out_specs=vmem,
        scratch_shapes=[
            pltpu.VMEM((rows + 4, ml, cols), F32),
            pltpu.VMEM((rows + 8, cols), F32),
            pltpu.VMEM((3, ml, cols), F32),
            pltpu.VMEM((2, ml, cols), F32),
            pltpu.VMEM((3, ml, cols), F32),
            pltpu.VMEM((2, ml, cols), F32),
            pltpu.VMEM((ng, nc, rc, ml, cc), F32),
            pltpu.VMEM((n_mem, rc, ml, cc), F32),
            pltpu.VMEM((n_mem, rc, ml, cc), F32),
            pltpu.VMEM((rows * ml, 2 * ob), F32),
            pltpu.VMEM((rows, 2 * ob), F32),
            pltpu.VMEM((n_mem, ml, ob), F32),
            pltpu.VMEM((n_slab, ml, ob), F32),
            pltpu.VMEM((n_slab, ml, ob), F32),
            pltpu.VMEM((n_slab, ml, members), F32),
            pltpu.VMEM((n_mem, ml, members), F32),
            dma((2,)), dma((2,)),
            dma((n_mem,)), dma((n_mem,)),
            dma((n_mem,)), dma((n_mem,)),
            dma((n_slab,)), dma((n_slab,)),
            dma((n_slab,)), dma((n_slab,)),
            dma((n_mem,)), dma((n_mem,)),
            dma((n_mem,)), dma((n_mem,)),
        ],
        compiler_params=pltpu.CompilerParams(collective_id=0, has_side_effects=True),
    )(
        thickness, face_u, face_v, obs_cells.T, obs_weights.T,
        obs_values.reshape(1, ob), obs_noise, cov_inverse, taper_mask,
    )
    return out.transpose(3, 0, 2, 1, 4).reshape(ml, rows, cols)


def solution(mesh):
    return jax.shard_map(
        functools.partial(local, mesh.shape["mem"], mesh.shape["slab"]),
        mesh=mesh,
        in_specs=(
            P("mem", "slab", None),
            P("slab", None),
            P("slab", None),
            P("slab", None),
            P("slab", None),
            P("slab"),
            P("mem", "slab"),
            P("slab", None),
            P(),
        ),
        out_specs=P("mem", "slab", None),
        check_vma=False,
    )
```

time: 139 us -> 53.3 us (0.38)
  the two profiles are of different devices: /device:TPU:0 before, /device:TPU:9 now
where the time goes in v1:
time: 53.3 us; the launch traced here: 53.1 us
  Pallas kernels  51 us (96%)
  local copies, waits for them, and re-layouts  2.17 us (4%)
    pallas_call x1, Pallas kernels, local(): pl.pallas_call(functools.partial(kernel, n_mem, n_slab, nc, rc), out_shap...  51 us
    reshape x1, local copies, waits for them, and re-layouts, local(): return out.transpose(3, 0, 2, 1, 4).reshape(ml, rows, cols)  2.17 us

profile of v1, /device:TPU:9, one launch (start us, length us, event | category | flops | bytes accessed | tf_op | source)
XLA Modules:
  0.0 53.1 jit_solution(5385122674007981943)
XLA Ops:
  0.0 51.0 %shard_map.91 = f32[8,1,8,8,384]{4,3,2,1,0:T(8,128)} custom-call(f32[8,64,384]{2,1,0:T(8,128)} %x_ref.1, f32[64,384]{1,0:T(8,128)} %u_ref.1, f32[64,384]{1,0:T(8,128)} %v_ref.1, s32[4,128]{1,0:T(4,128)} %bitcast.7, s32[4,128]{1,0:T(4,128)} %bitcast.8, f32[1,128]{1,0:T(1,128)} %bitcast.9, f32[8,128]{1,0:T(8,128)} %noise_ref.1, f32[128,512]{1,0:T(8,128)} %cinv_ref.1, ...), custom_call_target="tpu_custom_call" | custom-call | tf_op jit(solution)/shard_map/pallas_call | solution.py:284
  51.0 2.2 %copy.10 = f32[8,64,384]{2,1,0:T(8,128)} copy(f32[8,64,384]{2,0,1:T(8,128)} %bitcast.6) | data formatting | bytes 1572864 | tf_op jit(solution)/shard_map/reshape | solution.py:319

commit v2 on v1

--- a/solution.py
+++ b/solution.py
@@ -24,11 +24,11 @@
 
 
 def kernel(
-    n_mem, n_slab, nc, rc,
-    x_ref, u_ref, v_ref, cells_ref, wts_ref, vals_ref, noise_ref, cinv_ref, taper_ref,
+    n_mem, n_slab, nc, rc, ck,
+    x_hbm, u_ref, v_ref, cells_ref, wts_ref, vals_ref, noise_ref, cinv_hbm, taper_ref,
     res_ref,
     t_buf, v_buf, up_buf, dn_buf, hi_rx, lo_rx, fblk, gath, outb, s_buf, rw_buf,
-    om_all, p_buf, p_rx, b_buf, x_all,
+    om_all, p_buf, p_rx, b_buf, x_all, x_ref, cinv_ref, in_s,
     halo_s, halo_r, f_s, f_r, o_s, o_r, p_s, p_r, b_s, b_r, x_s, x_r, r_s, r_r,
 ):
     ng = n_mem // nc
@@ -44,12 +44,20 @@
     up = lax.rem(sl + 1, n_slab)
     down = lax.rem(sl + n_slab - 1, n_slab)
 
+    nch = rc // ck
+
+    x_in = pltpu.make_async_copy(x_hbm, x_ref, in_s.at[0])
+    cinv_in = pltpu.make_async_copy(cinv_hbm, cinv_ref, in_s.at[1])
+    x_in.start()
+    cinv_in.start()
+
     barrier = pltpu.get_barrier_semaphore()
     for k in range(1, n_mem):
         pl.semaphore_signal(barrier, inc=1, device_id=(lax.rem(me + k, n_mem), sl), device_id_type=MESH)
     for k in range(1, n_slab):
         pl.semaphore_signal(barrier, inc=1, device_id=(me, lax.rem(sl + k, n_slab)), device_id_type=MESH)
 
+    x_in.wait()
     tr = 8
 
     def load_rows(i, carry):
@@ -108,18 +116,21 @@
                 fblk[g, ci, r] = f[:, ci * cc:(ci + 1) * cc]
             h0, h1, s, flux = h1, h2, s1, flux1
 
-    def fwd_copy(g, ci, t, slot):
-        return pltpu.make_async_remote_copy(
-            src_ref=fblk.at[g, ci], dst_ref=gath.at[slot], send_sem=f_s.at[t], recv_sem=f_r.at[slot],
-            device_id=(t, sl), device_id_type=MESH)
-
-    def send_group(g):
+    def chunk(k):
+        return pl.ds(k * ck, ck)
+
+    def fwd_copy(k, g, ci, t, slot):
+        return pltpu.make_async_remote_copy(
+            src_ref=fblk.at[g, ci, chunk(k)], dst_ref=gath.at[slot, chunk(k)],
+            send_sem=f_s.at[k, t], recv_sem=f_r.at[k, slot], device_id=(t, sl), device_id_type=MESH)
+
+    def send_group(g, k):
         for ci in range(nc):
             t = g * nc + ci
 
             @pl.when(t != me)
             def _():
-                fwd_copy(g, ci, t, me).start()
+                fwd_copy(k, g, ci, t, me).start()
 
     def inner(k, carry):
         g = lax.rem(my_g + k, ng)
@@ -127,7 +138,7 @@
         @pl.when(jnp.logical_and(g >= 1, g <= ng - 2))
         def _():
             compute(g)
-            send_group(g)
+            send_group(g, 0)
 
         return carry
 
@@ -191,6 +202,7 @@
         bcast(om_all, me, t, t, sl, o_s, o_r).start()
 
     innovation = vals_ref[...] + noise_ref[...] - obs_model
+    cinv_in.wait()
     white_terms = jnp.dot(innovation, cinv_ref[...], preferred_element_type=F32, precision=lax.Precision.HIGHEST)
     for b in range(n_slab):
         p_buf[b] = white_terms[:, b * ob:(b + 1) * ob]
@@ -204,8 +216,15 @@
     for b in slab_mates:
         p_copy(b, sl).start()
 
-    send_group(0)
-    send_group(ng - 1)
+    send_group(0, 0)
+    send_group(ng - 1, 0)
+
+    def send_chunk(k):
+        for t in mem_mates:
+            fwd_copy(k, t // nc, t % nc, t, me).start()
+
+    if nch > 1:
+        send_chunk(1)
     gath[me] = fblk[my_g, my_c]
 
     for b in slab_mates:
@@ -232,29 +251,32 @@
     for t in mem_mates:
         bcast(x_all, me, t, t, sl, x_s, x_r).start()
 
-    for t in mem_mates:
-        fwd_copy(my_g, my_c, t, t).wait_recv()
+    for k in range(2, nch):
+        send_chunk(k)
+
     for t in mem_mates:
         bcast(x_all, t, t, t, sl, x_s, x_r).wait_recv()
-
     xm = x_all[...].reshape(members, members)
     x_hi = xm.astype(BF16).astype(F32)
     lhs = jnp.concatenate([x_hi, x_hi, xm - x_hi], axis=1).astype(BF16)
-    for r in range(rc):
-        g = gath[:, r].reshape(members, cc)
-        g_hi = g.astype(BF16)
-        g_lo = (g - g_hi.astype(F32)).astype(BF16)
-        rhs = jnp.concatenate([g_hi, g_lo, g_hi], axis=0)
-        out = g + jnp.dot(lhs, rhs, preferred_element_type=F32)
-        outb[:, r] = out.reshape(n_mem, ml, cc)
-
-    def rev_copy(t, g, ci, slot):
-        return pltpu.make_async_remote_copy(
-            src_ref=outb.at[t], dst_ref=res_ref.at[g, ci], send_sem=r_s.at[t], recv_sem=r_r.at[slot],
-            device_id=(t, sl), device_id_type=MESH)
-
-    for t in mem_mates:
-        rev_copy(t, my_g, my_c, me).start()
+
+    def rev_copy(k, t, g, ci, slot):
+        return pltpu.make_async_remote_copy(
+            src_ref=outb.at[t, chunk(k)], dst_ref=res_ref.at[g, ci, chunk(k)],
+            send_sem=r_s.at[k, t], recv_sem=r_r.at[k, slot], device_id=(t, sl), device_id_type=MESH)
+
+    for k in range(nch):
+        for t in mem_mates:
+            fwd_copy(k, my_g, my_c, t, t).wait_recv()
+        for r in range(k * ck, (k + 1) * ck):
+            g = gath[:, r].reshape(members, cc)
+            g_hi = g.astype(BF16)
+            g_lo = (g - g_hi.astype(F32)).astype(BF16)
+            rhs = jnp.concatenate([g_hi, g_lo, g_hi], axis=0)
+            out = g + jnp.dot(lhs, rhs, preferred_element_type=F32)
+            outb[:, r] = out.reshape(n_mem, ml, cc)
+        for t in mem_mates:
+            rev_copy(k, t, my_g, my_c, me).start()
     res_ref[my_g, my_c] = outb[me]
 
     to_down.wait_send()
@@ -265,11 +287,13 @@
     for t in mem_mates:
         bcast(om_all, me, t, t, sl, o_s, o_r).wait_send()
         bcast(x_all, me, t, t, sl, x_s, x_r).wait_send()
-        fwd_copy(t // nc, t % nc, t, me).wait_send()
-    for t in mem_mates:
-        rev_copy(t, my_g, my_c, me).wait_send()
-    for t in mem_mates:
-        rev_copy(t, t // nc, t % nc, t).wait_recv()
+        for k in range(nch):
+            fwd_copy(k, t // nc, t % nc, t, me).wait_send()
+    for k in range(nch):
+        for t in mem_mates:
+            rev_copy(k, t, my_g, my_c, me).wait_send()
+        for t in mem_mates:
+            rev_copy(k, t, t // nc, t % nc, t).wait_recv()
 
 
 def local(n_mem, n_slab, thickness, face_u, face_v, obs_cells, obs_weights, obs_values, obs_noise, cov_inverse,
@@ -279,12 +303,15 @@
     members = ml * n_mem
     nc, rc = split_blocks(rows, cols, n_mem)
     ng, cc = n_mem // nc, cols // nc
+    ck = rc // 4 if rc % 4 == 0 else rc
+    nch = rc // ck
     vmem = pl.BlockSpec(memory_space=pltpu.VMEM)
+    hbm = pl.BlockSpec(memory_space=pl.ANY)
     dma = pltpu.SemaphoreType.DMA
     out = pl.pallas_call(
-        functools.partial(kernel, n_mem, n_slab, nc, rc),
+        functools.partial(kernel, n_mem, n_slab, nc, rc, ck),
         out_shape=jax.ShapeDtypeStruct((ng, nc, rc, ml, cc), F32),
-        in_specs=[vmem] * 8 + [pl.BlockSpec(memory_space=pltpu.SMEM)],
+        in_specs=[hbm] + [vmem] * 6 + [hbm, pl.BlockSpec(memory_space=pltpu.SMEM)],
         out_specs=vmem,
         scratch_shapes=[
             pltpu.VMEM((rows + 4, ml, cols), F32),
@@ -303,13 +330,16 @@
             pltpu.VMEM((n_slab, ml, ob), F32),
             pltpu.VMEM((n_slab, ml, members), F32),
             pltpu.VMEM((n_mem, ml, members), F32),
+            pltpu.VMEM((ml, rows, cols), F32),
+            pltpu.VMEM((ob, n_slab * ob), F32),
+            dma((2,)),
             dma((2,)), dma((2,)),
-            dma((n_mem,)), dma((n_mem,)),
+            dma((nch, n_mem)), dma((nch, n_mem)),
             dma((n_mem,)), dma((n_mem,)),
             dma((n_slab,)), dma((n_slab,)),
             dma((n_slab,)), dma((n_slab,)),
             dma((n_mem,)), dma((n_mem,)),
-            dma((n_mem,)), dma((n_mem,)),
+            dma((nch, n_mem)), dma((nch, n_mem)),
         ],
         compiler_params=pltpu.CompilerParams(collective_id=0, has_side_effects=True),
     )(

time: 53.3 us -> 49.5 us (0.929)
  the two profiles are of different devices: /device:TPU:9 before, /device:TPU:0 now
where the time goes in v2:
time: 49.5 us; the launch traced here: 49.3 us
  Pallas kernels  47.2 us (95%)
  local copies, waits for them, and re-layouts  2.17 us (4%)
    pallas_call x1, Pallas kernels, local(): pl.pallas_call(functools.partial(kernel, n_mem, n_slab, nc, rc, ck), out_...  47.2 us
    reshape x1, local copies, waits for them, and re-layouts, local(): return out.transpose(3, 0, 2, 1, 4).reshape(ml, rows, cols)  2.17 us

profile of v2, /device:TPU:0, one launch (start us, length us, event | category | flops | bytes accessed | tf_op | source)
XLA Modules:
  0.0 49.3 jit_solution(10117676994558472571)
XLA Ops:
  0.0 47.2 %shard_map.91 = f32[8,1,8,8,384]{4,3,2,1,0:T(8,128)} custom-call(f32[8,64,384]{2,1,0:T(8,128)} %x_hbm.1, f32[64,384]{1,0:T(8,128)} %u_ref.1, f32[64,384]{1,0:T(8,128)} %v_ref.1, s32[4,128]{1,0:T(4,128)} %bitcast.7, s32[4,128]{1,0:T(4,128)} %bitcast.8, f32[1,128]{1,0:T(1,128)} %bitcast.9, f32[8,128]{1,0:T(8,128)} %noise_ref.1, f32[128,512]{1,0:T(8,128)} %cinv_hbm.1, ...), custom_call_target="tpu_custom_call" | custom-call | tf_op jit(solution)/shard_map/pallas_call | solution.py:311
  47.2 2.2 %copy.10 = f32[8,64,384]{2,1,0:T(8,128)} copy(f32[8,64,384]{2,0,1:T(8,128)} %bitcast.6) | data formatting | bytes 1572864 | tf_op jit(solution)/shard_map/reshape | solution.py:349

commit v3 on v2

--- a/solution.py
+++ b/solution.py
@@ -277,7 +277,9 @@
             outb[:, r] = out.reshape(n_mem, ml, cc)
         for t in mem_mates:
             rev_copy(k, t, my_g, my_c, me).start()
-    res_ref[my_g, my_c] = outb[me]
+    own = pltpu.make_async_copy(outb.at[me], res_ref.at[my_g, my_c], in_s.at[0])
+    own.start()
+    own.wait()
 
     to_down.wait_send()
     to_up.wait_send()
@@ -312,7 +314,7 @@
         functools.partial(kernel, n_mem, n_slab, nc, rc, ck),
         out_shape=jax.ShapeDtypeStruct((ng, nc, rc, ml, cc), F32),
         in_specs=[hbm] + [vmem] * 6 + [hbm, pl.BlockSpec(memory_space=pltpu.SMEM)],
-        out_specs=vmem,
+        out_specs=hbm,
         scratch_shapes=[
             pltpu.VMEM((rows + 4, ml, cols), F32),
             pltpu.VMEM((rows + 8, cols), F32),

time: 49.5 us -> 48.8 us (0.986)
  Pallas kernels: 47.2 us -> 46.4 us
    pallas_call x1, Pallas kernels: 47.2 us -> 46.4 us  [local(): pl.pallas_call(functools.partial(kernel, n_mem, n_slab, nc, rc, ck), out_...]
where the time goes in v3:
time: 48.8 us; the launch traced here: 48.6 us
  Pallas kernels  46.4 us (95%)
  local copies, waits for them, and re-layouts  2.17 us (4%)
    pallas_call x1, Pallas kernels, local(): pl.pallas_call(functools.partial(kernel, n_mem, n_slab, nc, rc, ck), out_...  46.4 us
    reshape x1, local copies, waits for them, and re-layouts, local(): return out.transpose(3, 0, 2, 1, 4).reshape(ml, rows, cols)  2.17 us

profile of v3, /device:TPU:0, one launch (start us, length us, event | category | flops | bytes accessed | tf_op | source)
XLA Modules:
  0.0 48.6 jit_solution(17892217587916238885)
XLA Ops:
  0.0 46.4 %shard_map.91 = f32[8,1,8,8,384]{4,3,2,1,0:T(8,128)} custom-call(f32[8,64,384]{2,1,0:T(8,128)} %x_hbm.1, f32[64,384]{1,0:T(8,128)} %u_ref.1, f32[64,384]{1,0:T(8,128)} %v_ref.1, s32[4,128]{1,0:T(4,128)} %bitcast.7, s32[4,128]{1,0:T(4,128)} %bitcast.8, f32[1,128]{1,0:T(1,128)} %bitcast.9, f32[8,128]{1,0:T(8,128)} %noise_ref.1, f32[128,512]{1,0:T(8,128)} %cinv_hbm.1, ...), custom_call_target="tpu_custom_call" | custom-call | tf_op jit(solution)/shard_map/pallas_call | solution.py:313
  46.4 2.2 %copy.10 = f32[8,64,384]{2,1,0:T(8,128)} copy(f32[8,64,384]{2,0,1:T(8,128)} %bitcast.6) | data formatting | bytes 1572864 | tf_op jit(solution)/shard_map/reshape | solution.py:351
